TPU v7x, 32 devices: a whole 2x2x4 slice. The times are simulated.
32 devices in a mesh: ctx: 8 (over z, y), fsdp: 4 (over x, core).
Axes of the slice: x: 2, y: 2, z: 4, core: 2. Of those that a mesh axis runs over, the one named last changes fastest.
Arguments:
- tokens: bfloat16 [4, 1024, 768], P('fsdp', 'ctx'), may hold values from -6 to 6
- first_gain: bfloat16 [768], P('fsdp'), may hold values from 0.5 to 1.5
- first_bias: bfloat16 [768], P('fsdp'), may hold values from -4 to 4
- attn_weight: bfloat16 [768, 2304], P('fsdp'), may hold values from -0.3125 to 0.3125
- query_bias: bfloat16 [768], P('fsdp'), may hold values from -4 to 4
- value_bias: bfloat16 [768], P('fsdp'), may hold values from -4 to 4
- proj_weight: bfloat16 [768, 768], P('fsdp'), may hold values from -6 to 6
- proj_bias: bfloat16 [768], P('fsdp'), may hold values from -6 to 6
- second_gain: bfloat16 [768], P('fsdp'), may hold values from 0.5 to 1.5
- second_bias: bfloat16 [768], P('fsdp'), may hold values from -4 to 4
- fc_weight: bfloat16 [768, 3072], P('fsdp'), may hold values from -0.21875 to 0.21875
- fc_bias: bfloat16 [3072], P('fsdp'), may hold values from -6 to 6
- out_weight: bfloat16 [3072, 768], P('fsdp'), may hold values from -0.3125 to 0.3125
- out_bias: bfloat16 [768], P('fsdp'), may hold values from -6 to 6
- cotangent: bfloat16 [4, 1024, 768], P('fsdp', 'ctx'), may hold values from -6 to 6
Outputs:
- block_out: bfloat16 [4, 1024, 768], P('fsdp', 'ctx')
- input_grad: bfloat16 [4, 1024, 768], P('fsdp', 'ctx')
- first_gain_grad: float32 [768], P('fsdp')
- first_bias_grad: float32 [768], P('fsdp')
- attn_weight_grad: float32 [768, 2304], P('fsdp')
- query_bias_grad: float32 [768], P('fsdp')
- value_bias_grad: float32 [768], P('fsdp')
- proj_weight_grad: float32 [768, 768], P('fsdp')
- proj_bias_grad: float32 [768], P('fsdp')
- second_gain_grad: float32 [768], P('fsdp')
- second_bias_grad: float32 [768], P('fsdp')
- fc_weight_grad: float32 [768, 3072], P('fsdp')
- fc_bias_grad: float32 [3072], P('fsdp')
- out_weight_grad: float32 [3072, 768], P('fsdp')
- out_bias_grad: float32 [768], P('fsdp')
All inputs are finite; a program needn't handle non-finite values.
Results may differ from a plain program's by a relative error of at most 0.017.
Values may be sent and summed in bfloat16 or wider, within the bound.
No kernel may reach another device: no remote copies, remote signals or barrier semaphores. Data moves between devices by JAX's collectives and lax.ppermute only.
A program may use at most 320 MiB of HBM per device.

v0:
```python
from functools import partial
import jax
import jax.numpy as jnp
from jax import lax
from jax.sharding import PartitionSpec as P

D = 768
H = 12
HD = 64
LAYERS = 12
EPSILON = 1e-05


def layer_norm(values_in, norm_gain, norm_shift):
    center = jnp.mean(values_in, axis=-1, keepdims=True)
    centered = values_in - center
    spread = jnp.mean(centered * centered, axis=-1, keepdims=True)
    return centered * lax.rsqrt(spread + EPSILON) * norm_gain + norm_shift


def left_product(first, second):
    return lax.dot_general(
        first, second, (((0,), (0,)), ((), ())), preferred_element_type=jnp.float32
    )


def right_product(first, second):
    return lax.dot_general(
        first, second, (((1,), (1,)), ((), ())), preferred_element_type=jnp.float32
    )


def score_block(query_rows, key_rows, query_offset, key_offset):
    scores = jnp.einsum(
        "sqhd,skhd->shqk", query_rows, key_rows, preferred_element_type=jnp.float32
    ) * HD ** (-0.5)
    query_index = query_offset + lax.broadcasted_iota(jnp.int32, (query_rows.shape[1], 1), 0)
    key_index = key_offset + lax.broadcasted_iota(jnp.int32, (1, key_rows.shape[1]), 1)
    return (scores, (key_index <= query_index)[None, None])


def pair_terms(
    query_rows, grad_rows, log_totals, deltas, key_rows, value_rows, query_offset, key_offset
):
    scores, visible = score_block(query_rows, key_rows, query_offset, key_offset)
    weights = jnp.where(visible, jnp.exp(scores - log_totals[..., None]), 0.0)
    grad_weights = jnp.einsum(
        "sqhd,skhd->shqk", grad_rows, value_rows, preferred_element_type=jnp.float32
    )
    grad_scores = (weights * (grad_weights - deltas[..., None])).astype(jnp.bfloat16)
    return (weights.astype(jnp.bfloat16), grad_scores)


def shards(
    tokens,
    first_gain,
    first_bias,
    attn_weight,
    query_bias,
    value_bias,
    proj_weight,
    proj_bias,
    second_gain,
    second_bias,
    fc_weight,
    fc_bias,
    out_weight,
    out_bias,
    cotangent,
):
    residual_scale = LAYERS ** (-0.5)
    score_scale = HD ** (-0.5)
    seq_count = tokens.shape[0]
    block_rows = tokens.shape[1]
    all_rows = seq_count * block_rows
    inputs = tokens.reshape(all_rows, D).astype(jnp.float32)
    ctx_index = lax.axis_index("ctx")
    my_offset = ctx_index * block_rows
    last_row = my_offset + block_rows - 1
    attn_gathered = (
        lax.all_gather(first_gain, "fsdp", axis=0, tiled=True),
        lax.all_gather(first_bias, "fsdp", axis=0, tiled=True),
        lax.all_gather(attn_weight, "fsdp", axis=0, tiled=True),
        lax.all_gather(query_bias, "fsdp", axis=0, tiled=True),
        lax.all_gather(value_bias, "fsdp", axis=0, tiled=True),
        lax.all_gather(proj_weight, "fsdp", axis=0, tiled=True),
        lax.all_gather(proj_bias, "fsdp", axis=0, tiled=True),
    )
    gain_one, shift_one, attn_matrix, query_shift, value_shift, proj_matrix, proj_shift = (
        attn_gathered
    )
    gain_one = gain_one.astype(jnp.float32)
    shift_one = shift_one.astype(jnp.float32)
    normed = layer_norm(inputs, gain_one, shift_one).astype(jnp.bfloat16)
    mixed_rows = jnp.dot(normed, attn_matrix, preferred_element_type=jnp.float32)
    query_flat = (
        (mixed_rows[:, :D] + query_shift.astype(jnp.float32))
        .astype(jnp.bfloat16)
        .reshape(seq_count, block_rows, D)
    )
    key_flat = mixed_rows[:, D : 2 * D].astype(jnp.bfloat16).reshape(seq_count, block_rows, D)
    value_flat = (
        (mixed_rows[:, 2 * D :] + value_shift.astype(jnp.float32))
        .astype(jnp.bfloat16)
        .reshape(seq_count, block_rows, D)
    )
    query_heads = query_flat.reshape(seq_count, block_rows, H, HD)
    start_state = (
        jnp.full((seq_count, H, block_rows), -1e30, jnp.float32),
        jnp.zeros((seq_count, H, block_rows), jnp.float32),
        jnp.zeros((seq_count, H, block_rows, HD), jnp.float32),
    )
    offset = jnp.int32(0)
    key_rows = lax.all_gather(key_flat, "ctx", axis=1, tiled=True)
    value_rows = lax.all_gather(value_flat, "ctx", axis=1, tiled=True)
    row_count = key_rows.shape[1]

    def update(running):
        running_max, running_sum, running_acc = running
        scores, visible = score_block(
            query_heads, key_rows.reshape(seq_count, row_count, H, HD), my_offset, offset
        )
        scores = jnp.where(visible, scores, -1e30)
        new_max = jnp.maximum(running_max, jnp.max(scores, axis=-1))
        weights = jnp.where(visible, jnp.exp(scores - new_max[..., None]), 0.0)
        running_acc = jnp.einsum(
            "shqk,skhd->shqd",
            weights.astype(jnp.bfloat16),
            value_rows.reshape(seq_count, row_count, H, HD),
            preferred_element_type=jnp.float32,
        )
        running_sum = jnp.sum(weights, axis=-1)
        return (new_max, running_sum, running_acc)

    final_max, final_sum, final_acc = lax.cond(
        offset <= last_row, update, lambda unchanged: unchanged, start_state
    )
    log_totals = final_max + jnp.log(final_sum)
    attended_heads = final_acc / final_sum[..., None]
    attended_exact = attended_heads.transpose(0, 2, 1, 3).reshape(all_rows, D)
    attended = attended_exact.astype(jnp.bfloat16)
    branch = jnp.dot(attended, proj_matrix, preferred_element_type=jnp.float32) + proj_shift.astype(
        jnp.float32
    )
    middle = inputs + residual_scale * branch
    mlp_gathered = (
        lax.all_gather(second_gain, "fsdp", axis=0, tiled=True),
        lax.all_gather(second_bias, "fsdp", axis=0, tiled=True),
        lax.all_gather(fc_weight, "fsdp", axis=0, tiled=True),
        lax.all_gather(fc_bias, "fsdp", axis=0, tiled=True),
        lax.all_gather(out_weight, "fsdp", axis=0, tiled=True),
        lax.all_gather(out_bias, "fsdp", axis=0, tiled=True),
    )
    gain_two, shift_two, fc_matrix, fc_shift, out_matrix, out_shift = mlp_gathered
    gain_two = gain_two.astype(jnp.float32)
    shift_two = shift_two.astype(jnp.float32)
    normed_two = layer_norm(middle, gain_two, shift_two).astype(jnp.bfloat16)
    hidden = jnp.dot(normed_two, fc_matrix, preferred_element_type=jnp.float32) + fc_shift.astype(
        jnp.float32
    )
    gelu_fn = partial(jax.nn.gelu, approximate=True)
    active_exact, gelu_back = jax.vjp(gelu_fn, hidden)
    active = active_exact.astype(jnp.bfloat16)
    output = jnp.dot(active, out_matrix, preferred_element_type=jnp.float32) + out_shift.astype(
        jnp.float32
    )
    block_out = (middle + residual_scale * output).astype(jnp.bfloat16)
    grad_rows = cotangent.reshape(all_rows, D).astype(jnp.float32)
    grad_output = (residual_scale * grad_rows).astype(jnp.bfloat16)
    out_weight_grad = left_product(active, grad_output)
    out_bias_grad = jnp.sum(grad_output.astype(jnp.float32), axis=0)
    grad_active = right_product(grad_output, out_matrix)
    grad_hidden = gelu_back(grad_active)[0].astype(jnp.bfloat16)
    fc_weight_grad = left_product(normed_two, grad_hidden)
    fc_bias_grad = jnp.sum(grad_hidden.astype(jnp.float32), axis=0)
    grad_normed_two = right_product(grad_hidden, fc_matrix)
    norm_two_value, norm_two_back = jax.vjp(layer_norm, middle, gain_two, shift_two)
    grad_middle, second_gain_grad, second_bias_grad = norm_two_back(grad_normed_two)
    grad_middle = grad_middle + grad_rows
    grad_branch = (residual_scale * grad_middle).astype(jnp.bfloat16)
    proj_weight_grad = left_product(attended, grad_branch)
    proj_bias_grad = jnp.sum(grad_branch.astype(jnp.float32), axis=0)
    grad_attended = right_product(grad_branch, proj_matrix).astype(jnp.bfloat16)
    grad_heads = grad_attended.reshape(seq_count, block_rows, H, HD)
    grad_seq = grad_attended.reshape(seq_count, block_rows, D)
    deltas = jnp.sum(grad_heads.astype(jnp.float32).transpose(0, 2, 1, 3) * attended_heads, axis=-1)
    zero_flat = jnp.zeros((seq_count, block_rows, D), jnp.float32)
    zero_heads = jnp.zeros((seq_count, block_rows, H, HD), jnp.float32)
    all_totals, all_deltas = (
        lax.all_gather(log_totals, "ctx", axis=2, tiled=True),
        lax.all_gather(deltas, "ctx", axis=2, tiled=True),
    )
    key_heads_own = key_flat.reshape(seq_count, block_rows, H, HD)
    value_heads_own = value_flat.reshape(seq_count, block_rows, H, HD)

    def key_side(carried, arrived, offset):
        query_rows, grad_piece = arrived
        row_count = query_rows.shape[1]

        def key_visit_block(partials):
            query_part = query_rows.reshape(seq_count, row_count, H, HD)
            grad_part = grad_piece.reshape(seq_count, row_count, H, HD)
            weights, grad_scores = pair_terms(
                query_part,
                grad_part,
                all_totals,
                all_deltas,
                key_heads_own,
                value_heads_own,
                offset,
                my_offset,
            )
            key_sum = score_scale * jnp.einsum(
                "shqk,sqhd->skhd", grad_scores, query_part, preferred_element_type=jnp.float32
            ).reshape(seq_count, block_rows, D)
            value_sum = jnp.einsum(
                "shqk,sqhd->skhd", weights, grad_part, preferred_element_type=jnp.float32
            ).reshape(seq_count, block_rows, D)
            return (key_sum, value_sum)

        return lax.cond(
            offset + row_count - 1 >= my_offset,
            key_visit_block,
            lambda unchanged: unchanged,
            carried,
        )

    key_grad, value_grad = key_side(
        (zero_flat, zero_flat),
        (
            lax.all_gather(query_flat, "ctx", axis=1, tiled=True),
            lax.all_gather(grad_seq, "ctx", axis=1, tiled=True),
        ),
        jnp.int32(0),
    )

    def query_side(carried, arrived, offset):
        key_rows, value_rows = arrived
        row_count = key_rows.shape[1]

        def query_visit_block(query_sum):
            key_part = key_rows.reshape(seq_count, row_count, H, HD)
            weights, grad_scores = pair_terms(
                query_heads,
                grad_heads,
                log_totals,
                deltas,
                key_part,
                value_rows.reshape(seq_count, row_count, H, HD),
                my_offset,
                offset,
            )
            return score_scale * jnp.einsum(
                "shqk,skhd->sqhd", grad_scores, key_part, preferred_element_type=jnp.float32
            )

        return lax.cond(offset <= last_row, query_visit_block, lambda unchanged: unchanged, carried)

    query_grad = query_side(
        zero_heads,
        (
            lax.all_gather(key_flat, "ctx", axis=1, tiled=True),
            lax.all_gather(value_flat, "ctx", axis=1, tiled=True),
        ),
        jnp.int32(0),
    )
    grad_mixed = jnp.concatenate(
        [
            query_grad.reshape(all_rows, D).astype(jnp.bfloat16),
            key_grad.reshape(all_rows, D).astype(jnp.bfloat16),
            value_grad.reshape(all_rows, D).astype(jnp.bfloat16),
        ],
        axis=1,
    )
    attn_weight_grad = left_product(normed, grad_mixed)
    query_bias_grad = jnp.sum(grad_mixed[:, :D].astype(jnp.float32), axis=0)
    value_bias_grad = jnp.sum(grad_mixed[:, 2 * D :].astype(jnp.float32), axis=0)
    grad_normed = right_product(grad_mixed, attn_matrix)
    norm_one_value, norm_one_back = jax.vjp(layer_norm, inputs, gain_one, shift_one)
    grad_inputs, first_gain_grad, first_bias_grad = norm_one_back(grad_normed)
    input_grad = (grad_inputs + grad_middle).astype(jnp.bfloat16)
    owned = (
        lax.psum_scatter(
            first_gain_grad.astype(jnp.bfloat16), "fsdp", scatter_dimension=0, tiled=True
        ).astype(jnp.float32),
        lax.psum_scatter(
            first_bias_grad.astype(jnp.bfloat16), "fsdp", scatter_dimension=0, tiled=True
        ).astype(jnp.float32),
        lax.psum_scatter(
            attn_weight_grad.astype(jnp.bfloat16), "fsdp", scatter_dimension=0, tiled=True
        ).astype(jnp.float32),
        lax.psum_scatter(
            query_bias_grad.astype(jnp.bfloat16), "fsdp", scatter_dimension=0, tiled=True
        ).astype(jnp.float32),
        lax.psum_scatter(
            value_bias_grad.astype(jnp.bfloat16), "fsdp", scatter_dimension=0, tiled=True
        ).astype(jnp.float32),
        lax.psum_scatter(
            proj_weight_grad.astype(jnp.bfloat16), "fsdp", scatter_dimension=0, tiled=True
        ).astype(jnp.float32),
        lax.psum_scatter(
            proj_bias_grad.astype(jnp.bfloat16), "fsdp", scatter_dimension=0, tiled=True
        ).astype(jnp.float32),
        lax.psum_scatter(
            second_gain_grad.astype(jnp.bfloat16), "fsdp", scatter_dimension=0, tiled=True
        ).astype(jnp.float32),
        lax.psum_scatter(
            second_bias_grad.astype(jnp.bfloat16), "fsdp", scatter_dimension=0, tiled=True
        ).astype(jnp.float32),
        lax.psum_scatter(
            fc_weight_grad.astype(jnp.bfloat16), "fsdp", scatter_dimension=0, tiled=True
        ).astype(jnp.float32),
        lax.psum_scatter(
            fc_bias_grad.astype(jnp.bfloat16), "fsdp", scatter_dimension=0, tiled=True
        ).astype(jnp.float32),
        lax.psum_scatter(
            out_weight_grad.astype(jnp.bfloat16), "fsdp", scatter_dimension=0, tiled=True
        ).astype(jnp.float32),
        lax.psum_scatter(
            out_bias_grad.astype(jnp.bfloat16), "fsdp", scatter_dimension=0, tiled=True
        ).astype(jnp.float32),
    )
    summed = lax.psum(
        (
            owned[0],
            owned[1],
            owned[2],
            owned[3],
            owned[4],
            owned[5],
            owned[6],
            owned[7],
            owned[8],
            owned[9],
            owned[10],
            owned[11],
            owned[12],
        ),
        "ctx",
    )
    return (
        block_out.reshape(seq_count, block_rows, D),
        input_grad.reshape(seq_count, block_rows, D),
        summed[0],
        summed[1],
        summed[2],
        summed[3],
        summed[4],
        summed[5],
        summed[6],
        summed[7],
        summed[8],
        summed[9],
        summed[10],
        summed[11],
        summed[12],
    )


def solution(mesh):
    placed = (
        P("fsdp", "ctx", None),
        P("fsdp"),
        P("fsdp"),
        P("fsdp", None),
        P("fsdp"),
        P("fsdp"),
        P("fsdp", None),
        P("fsdp"),
        P("fsdp"),
        P("fsdp"),
        P("fsdp", None),
        P("fsdp"),
        P("fsdp", None),
        P("fsdp"),
        P("fsdp", "ctx", None),
    )
    return jax.shard_map(
        shards,
        mesh=mesh,
        in_specs=placed,
        out_specs=(
            P("fsdp", "ctx", None),
            P("fsdp", "ctx", None),
            P("fsdp"),
            P("fsdp"),
            P("fsdp", None),
            P("fsdp"),
            P("fsdp"),
            P("fsdp", None),
            P("fsdp"),
            P("fsdp"),
            P("fsdp"),
            P("fsdp", None),
            P("fsdp"),
            P("fsdp", None),
            P("fsdp"),
        ),
        check_vma=False,
    )
```

profile of v0, /device:TPU:0, one launch (start us, length us, event | category | flops | bytes accessed | tf_op | source)
XLA Modules:
  0.0 782.9 jit_solution(8197349530382373933)
XLA Ops:
  7.2 0.7 all-gather.15.cloned.1.call-update
  8.0 1.3 fusion.91
  10.0 0.8 dynamic-update-slice
  10.8 0.8 dynamic-update-slice.1
  11.6 0.8 dynamic-update-slice.2
  12.5 0.8 dynamic-update-slice.3
  13.3 0.8 dynamic-update-slice.4
  14.2 0.8 dynamic-update-slice.5
  15.0 0.8 dynamic-update-slice.6
  15.8 13.4 %all-reduce.19 = (bf16[768]{0:T(1024)(128)(2,1)S(1)}, bf16[768]{0:T(1024)(128)(2,1)S(1)}, bf16[768]{0:T(1024)(128)(2,1)S(1)}, bf16[768]{0:T(1024)(128)(2,1)S(1)}...) all-reduce(bf16[768]{0:T(1024)(128)(2,1)S(1)} %dynamic-update-slice, ...), channel_id=1, replica_groups=mesh['ctx'=8,'fsdp'=4] {'fsdp'}, use_global_device_ids=true, to_apply=%add.1 | all-reduce | flops 5376 | bytes 21504
  29.2 1.0 convert_reduce_fusion
  30.3 1.1 fusion.63
  31.4 11.8 %all-gather.15.cloned.1.call-done = bf16[768,2304]{1,0:T(8,128)(2,1)} async-done(((bf16[192,2304]{1,0:T(8,128)(2,1)}), bf16[768,2304]{1,0:T(8,128)(2,1)}) %all-gather.15.cloned.1.call-update) | async-done | bytes 3538960 | tf_op jit(solution)/shard_map/all_gather | solution.py:83
  43.2 2.8 fusion.85
  46.1 0.7 fusion.66
  46.9 0.7 slice.23
  49.5 5.2 all-gather.5
  54.7 0.8 copy.51
  55.7 35.5 %all-gather.25.cloned.1.call-done = bf16[1024,768]{1,0:T(8,128)(2,1)} async-done(((bf16[128,768]{1,0:T(8,128)(2,1)}), bf16[1024,768]{1,0:T(8,128)(2,1)}) %all-gather.25.cloned.1.call-update) | async-done | bytes 1572880 | tf_op jit(solution)/shard_map/all_gather | solution.py:115
  91.3 45.8 %all-gather.23.cloned.1.call-done = bf16[1024,768]{1,0:T(8,128)(2,1)} async-done(((bf16[128,768]{1,0:T(8,128)(2,1)}), bf16[1024,768]{1,0:T(8,128)(2,1)}) %all-gather.23.cloned.1.call-update) | async-done | bytes 1572880 | tf_op jit(solution)/shard_map/all_gather | solution.py:114
  137.1 13.5 %conditional.3 = (f32[1,12,128]{2,1,0:T(8,128)S(1)}, f32[1,12,128,64]{2,3,1,0:T(8,128)S(1)}, f32[1,12,128]{2,1,0:T(8,128)S(1)}) conditional(s32[]{:T(128)} %convert_element_type.215, () %tuple.32, (s32[]{:T(128)}, bf16[1,128,12,64]{1,3,2,0:T(8,128)(2,1)}, bf16[1,1024,768]{2,1,0:T(8,128)(2,1)}, bf16[1,1024,768]{2,1,0:T(8,128)(2,1)}) %tuple.106), branch_computations={%region_2.0_spmd.clone, %region_3.6_spmd.clone} | conditional | flops 423233152 | bytes 60988556 | solution.py:135
  137.2 1.7 copy.61
  138.9 2.2 fusion.26
  141.2 2.0 fusion.28
  143.2 0.8 copy-done
  144.0 1.6 copy.62
  145.6 4.9 fusion.32
  150.6 4.1 all-gather.17.cloned.1.call-done
  154.8 1.7 fusion.92
  156.7 36.9 %all-gather.19.cloned.1.call-done = bf16[768,3072]{1,0:T(8,128)(2,1)} async-done(((bf16[192,3072]{1,0:T(8,128)(2,1)}), bf16[768,3072]{1,0:T(8,128)(2,1)}) %all-gather.19.cloned.1.call-update) | async-done | bytes 4718608 | tf_op jit(solution)/shard_map/all_gather | solution.py:149
  193.7 3.2 convolution_add_fusion
  196.9 35.7 %all-gather.21.cloned.1.call-done = bf16[3072,768]{1,0:T(8,128)(2,1)} async-done(((bf16[768,768]{1,0:T(8,128)(2,1)}), bf16[3072,768]{1,0:T(8,128)(2,1)}) %all-gather.21.cloned.1.call-update) | async-done | bytes 4718608 | tf_op jit(solution)/shard_map/all_gather | solution.py:151
  232.6 5.0 fusion.93
  237.6 2.3 multiply_reduce_fusion
  240.8 0.7 fusion.89
  241.6 1.2 convolution_convert_fusion.4
  242.9 1.5 convolution_convert_fusion.3
  244.4 4.9 convolution_convert_fusion.1
  249.6 3.8 convolution_convert_fusion
  253.5 0.8 copy-done.9
  255.2 17.2 %conditional.4 = (bf16[1,128,12,64]{1,3,2,0:T(8,128)(2,1)S(1)}) conditional(s32[]{:T(128)} %convert_element_type.215, () %tuple.34, (s32[]{:T(128)}, bf16[1,128,12,64]{1,3,2,0:T(8,128)(2,1)}, bf16[1,1024,768]{2,1,0:T(8,128)(2,1)}, f32[1,12,128]{2,1,0:T(8,128)}, bf16[1,128,12,64]{1,3,2,0:T(8,128)(2,1)}, /*index=5*/bf16[1,1024,768]{2,1,0:T(8,128)(2,1)}, ...), branch_computations={%region_11.12_spmd, %region_12.13_spmd} | conditional | flops 613744768 | bytes 25269316 | solution.py:257
  255.2 2.6 copy.55
  257.8 5.2 fusion.8
  263.0 2.6 copy.56
  265.8 6.6 fusion.5
  272.4 32.5 %all-gather.4 = f32[12,1024]{1,0:T(8,128)} all-gather(f32[12,128]{1,0:T(8,128)S(1)} %fusion.68), channel_id=6, replica_groups=mesh['ctx'=8,'fsdp'=4] {'ctx'}, dimensions={1}, use_global_device_ids=true | all-gather | bytes 55296 | tf_op jit(solution)/shard_map/all_gather | solution.py:191
  304.9 33.0 %all_gather.75 = f32[1,12,1024]{2,1,0:T(8,128)} all-gather(f32[1,12,128]{2,1,0:T(8,128)} %copy-done.22), channel_id=1, replica_groups=mesh['ctx'=8,'fsdp'=4] {'ctx'}, dimensions={2}, use_global_device_ids=true | all-gather | bytes 55296 | tf_op jit(solution)/shard_map/all_gather | solution.py:190
  338.0 23.5 %conditional.5 = (bf16[1,128,768]{1,2,0:T(8,128)(2,1)S(1)}, bf16[128,768]{0,1:T(8,128)(2,1)S(1)}) conditional(s32[]{:T(128)} %convert_element_type.242, () %tuple.36, (s32[]{:T(128)}, bf16[1,1024,768]{2,1,0:T(8,128)(2,1)}, bf16[128,768]{1,0:T(8,128)(2,1)S(1)}, f32[1,12,1024]{2,1,0:T(8,128)}, bf16[1,1024,768]{2,1,0:T(8,128)(2,1)}, ...), branch_computations={%region_13.14_spmd, %region_14.15_spmd} | conditional | flops 821362816 | bytes 33965132 | solution.py:221
  338.0 2.6 copy.57
  340.7 5.1 fusion.94
  345.9 2.6 copy.59
  348.7 8.3 %fusion.21 = bf16[12,128,64]{1,2,0:T(8,128)(2,1)S(1)} fusion(bf16[1024,12,64]{0,2,1:T(8,128)(2,1)} %bitcast.164, f32[12,1024,128]{2,1,0:T(8,128)} %fusion.94, f32[12,1024]{1,0:T(8,128)S(1)} %bitcast.189, f32[12,1024]{1,0:T(8,128)} %bitcast.190, pred[1024,128]{1,0:T(8,128)(4,1)S(1)} %iota_compare_fusion.1, bf16[1024,12,64]{0,2,1:T(8,128)(2,1)} %bitcast.176, ...), kind=kOutput, calls=%fused_computation.22 | convolution fusion | flops 412286976 | bytes 10059776 | tf_op jit(solution)/shard_map/cond/branch_1_fun/shqk,sqhd->skhd/dot_general | solution.py:213
  357.0 4.4 fusion.13
  361.5 3.3 convolution_convert_fusion.2
  366.8 1.3 dynamic-update-slice.7
  369.0 0.7 convert_reduce_fusion.1
  369.7 4.1 fusion.88
  374.1 12.4 %all-reduce.18 = (bf16[768]{0:T(1024)(128)(2,1)S(1)}, bf16[768]{0:T(1024)(128)(2,1)S(1)}, bf16[768]{0:T(1024)(128)(2,1)S(1)}, bf16[768]{0:T(1024)(128)(2,1)S(1)}...) all-reduce(bf16[768]{0:T(1024)(128)(2,1)} %dynamic-update-slice.7, ...), channel_id=1, replica_groups=mesh['ctx'=8,'fsdp'=4] {'fsdp'}, use_global_device_ids=true, to_apply=%add.7 | all-reduce | flops 9984 | bytes 39936
  386.9 1.6 fusion.70
  388.5 4.1 fusion.52
  392.6 10.9 %reduce-scatter.9.cloned.1.call-done = bf16[192,3072]{1,0:T(8,128)(2,1)} async-done(((bf16[768,3072]{1,0:T(8,128)(2,1)}), bf16[192,3072]{1,0:T(8,128)(2,1)}) %reduce-scatter.9.cloned.1.call-update) | async-done | bytes 1179664 | tf_op jit(solution)/shard_map/reduce_scatter | solution.py:310
  403.5 50.4 %reduce-scatter.11.cloned.1.call-done = bf16[768,768]{1,0:T(8,128)(2,1)} async-done(((bf16[3072,768]{1,0:T(8,128)(2,1)}), bf16[768,768]{1,0:T(8,128)(2,1)}) %reduce-scatter.11.cloned.1.call-update) | async-done | bytes 1179664 | tf_op jit(solution)/shard_map/reduce_scatter | solution.py:316
  453.9 43.0 %reduce-scatter.5.cloned.1.call-done = bf16[192,2304]{1,0:T(8,128)(2,1)} async-done(((bf16[768,2304]{1,0:T(8,128)(2,1)}), bf16[192,2304]{1,0:T(8,128)(2,1)}) %reduce-scatter.5.cloned.1.call-update) | async-done | bytes 884752 | tf_op jit(solution)/shard_map/reduce_scatter | solution.py:289
  497.0 279.1 %all-reduce.21 = (f32[192]{0:T(256)}, f32[192]{0:T(256)}, f32[192,2304]{1,0:T(8,128)}, f32[192]{0:T(256)}, f32[192]{0:T(256)}, /*index=5*/f32[192,768]{1,0:T(8,1...) all-reduce(f32[192]{0:T(256)S(1)} %get-tuple-element.212, ...), channel_id=1, replica_groups=mesh['ctx'=8,'fsdp'=4] {'ctx'}, use_global_device_ids=true, to_apply=%region_19.20 | all-reduce | flops 1771776 | bytes 10635264 | tf_op jit(solution)/shard_map/psum | solution.py:323
  (145 shorter events, 7.5 us)
Async XLA Ops:
  7.2 36.1 %all-gather.15.cloned.1.call-start = ((), (), s32[]{:S(2)}) async-start(), calls=%async_computation.4 | async-start | bytes 4423680 | tf_op jit(solution)/shard_map/all_gather | solution.py:83
  7.9 83.4 %all-gather.25.cloned.1.call-start = ((), (), s32[]{:S(2)}) async-start(), calls=%async_computation.13 | async-start | bytes 1769472 | tf_op jit(solution)/shard_map/all_gather | solution.py:115
  30.2 15.8 %copy-start.25 = (f32[128]{0:T(128)}, f32[128]{0:T(128)S(1)}, u32[]{:S(2)}) copy-start(f32[128]{0:T(128)S(1)} %broadcast_multiply_fusion.1) | copy-start | bytes 1540
  31.4 14.7 %copy-start.33 = (f32[128]{0:T(128)}, f32[128]{0:T(128)S(1)}, u32[]{:S(2)}) copy-start(f32[128]{0:T(128)S(1)} %fusion.63) | copy-start | bytes 1540
  31.4 14.7 %copy-start.28 = (f32[128]{0:T(128)}, f32[128]{0:T(128)S(1)}, u32[]{:S(2)}) copy-start(f32[128]{0:T(128)S(1)} %fusion.78) | copy-start | bytes 1540
  46.8 7.8 %copy-start.8 = (bf16[128,768]{1,0:T(8,128)(2,1)}, bf16[128,768]{1,0:T(8,128)(2,1)S(1)}, u32[]{:S(2)}) copy-start(bf16[128,768]{1,0:T(8,128)(2,1)S(1)} %get-tuple-element.195) | copy-start | bytes 589828
  46.8 2.6 copy-start.32
  46.9 90.2 %all-gather.23.cloned.1.call-start = ((), (), s32[]{:S(2)}) async-start(), calls=%async_computation.12 | async-start | bytes 1769472 | tf_op jit(solution)/shard_map/all_gather | solution.py:114
  47.6 107.1 %all-gather.17.cloned.1.call-start = ((), (), s32[]{:S(2)}) async-start(), calls=%async_computation.5 | async-start | bytes 1474560 | tf_op jit(solution)/shard_map/all_gather | solution.py:86
  48.2 145.5 %all-gather.19.cloned.1.call-start = ((), (), s32[]{:S(2)}) async-start(), calls=%async_computation.6 | async-start | bytes 5898240 | tf_op jit(solution)/shard_map/all_gather | solution.py:149
  48.8 183.8 %all-gather.21.cloned.1.call-start = ((), (), s32[]{:S(2)}) async-start(), calls=%async_computation.7 | async-start | bytes 5898240 | tf_op jit(solution)/shard_map/all_gather | solution.py:151
  49.4 288.5 %all-gather.27.cloned.1.call-start = ((), (), s32[]{:S(2)}) async-start(), calls=%async_computation.14 | async-start | bytes 1769472 | tf_op jit(solution)/shard_map/all_gather | solution.py:231
  55.5 282.4 %all-gather.29.cloned.1.call-start = ((), (), s32[]{:S(2)}) async-start(), calls=%async_computation.15 | async-start | bytes 1769472 | tf_op jit(solution)/shard_map/all_gather | solution.py:232
  137.1 17.7 %copy-start.2 = (bf16[1,128,768]{2,1,0:T(8,128)(2,1)S(1)}, bf16[1,128,768]{2,1,0:T(8,128)(2,1)}, u32[]{:S(2)}) copy-start(bf16[1,128,768]{2,1,0:T(8,128)(2,1)} %param.21) | copy-start | bytes 589828
  141.2 2.8 copy-start
  141.2 2.8 copy-start.3
  144.0 1.6 copy-start.16
  145.6 5.0 copy-start.17
  150.6 43.1 %copy-start.18 = (f32[1,12,128]{2,1,0:T(8,128)}, f32[1,12,128]{2,1,0:T(8,128)S(1)}, u32[]{:S(2)}) copy-start(f32[1,12,128]{2,1,0:T(8,128)S(1)} %get-tuple-element.81) | copy-start | bytes 18436
  150.6 43.1 %copy-start.22 = (f32[1,12,128]{2,1,0:T(8,128)}, f32[1,12,128]{2,1,0:T(8,128)S(1)}, u32[]{:S(2)}) copy-start(f32[1,12,128]{2,1,0:T(8,128)S(1)} %get-tuple-element.140) | copy-start | bytes 18436
  156.5 83.4 %copy-start.24 = (f32[128]{0:T(128)}, f32[128]{0:T(128)S(1)}, u32[]{:S(2)}) copy-start(f32[128]{0:T(128)S(1)} %broadcast_multiply_fusion) | copy-start | bytes 1540
  156.7 83.2 %copy-start.27 = (f32[128]{0:T(128)}, f32[128]{0:T(128)S(1)}, u32[]{:S(2)}) copy-start(f32[128]{0:T(128)S(1)} %fusion.79) | copy-start | bytes 1540
  193.7 38.9 %copy-start.10 = (bf16[1,128,768]{2,1,0:T(8,128)(2,1)S(1)}, bf16[1,128,768]{2,1,0:T(8,128)(2,1)}, u32[]{:S(2)}) copy-start(bf16[1,128,768]{2,1,0:T(8,128)(2,1)} %param.35) | copy-start | bytes 589828
  232.6 5.1 copy-start.1
  237.6 2.3 copy-start.5
  239.9 1.6 copy-start.4
  240.2 0.6 copy-start.31
  242.8 126.1 %reduce-scatter.7.cloned.1.call-start = ((), (), s32[]{:S(2)}) async-start(), calls=%async_computation.9 | async-start | bytes 1474560 | tf_op jit(solution)/shard_map/reduce_scatter | solution.py:298
  244.4 159.2 %reduce-scatter.9.cloned.1.call-start = ((), (), s32[]{:S(2)}) async-start(), calls=%async_computation.10 | async-start | bytes 5898240 | tf_op jit(solution)/shard_map/reduce_scatter | solution.py:310
  249.3 204.6 %reduce-scatter.11.cloned.1.call-start = ((), (), s32[]{:S(2)}) async-start(), calls=%async_computation.11 | async-start | bytes 5898240 | tf_op jit(solution)/shard_map/reduce_scatter | solution.py:316
  253.4 0.9 copy-start.9
  253.4 1.1 copy-start.19
  253.4 243.6 %reduce-scatter.5.cloned.1.call-start = ((), (), s32[]{:S(2)}) async-start(), calls=%async_computation.8 | async-start | bytes 4423680 | tf_op jit(solution)/shard_map/reduce_scatter | solution.py:289
  254.5 0.7 copy-start.13
  255.2 82.8 %copy-start.6 = (bf16[128,768]{1,0:T(8,128)(2,1)S(1)}, bf16[128,768]{1,0:T(8,128)(2,1)}, u32[]{:S(2)}) copy-start(bf16[128,768]{1,0:T(8,128)(2,1)} %get-tuple-element.194) | copy-start | bytes 589828
  255.2 82.8 %copy-start.7 = (bf16[128,768]{1,0:T(8,128)(2,1)S(1)}, bf16[128,768]{1,0:T(8,128)(2,1)}, u32[]{:S(2)}) copy-start(bf16[128,768]{1,0:T(8,128)(2,1)} %slice.23) | copy-start | bytes 589828
  263.0 2.8 copy-start.14
  263.0 2.8 copy-start.23
  337.9 23.6 %copy-start.26 = (f32[128]{0:T(128)S(1)}, f32[128]{0:T(128)}, u32[]{:S(2)}) copy-start(f32[128]{0:T(128)} %copy-done.25) | copy-start | bytes 1540
  337.9 23.6 %copy-start.29 = (f32[128]{0:T(128)S(1)}, f32[128]{0:T(128)}, u32[]{:S(2)}) copy-start(f32[128]{0:T(128)} %copy-done.28) | copy-start | bytes 1540
  345.9 2.9 copy-start.20
  348.7 8.3 %copy-start.21 = (f32[1,12,1024]{2,1,0:T(8,128)S(1)}, f32[1,12,1024]{2,1,0:T(8,128)}, u32[]{:S(2)}) copy-start(f32[1,12,1024]{2,1,0:T(8,128)} %get-tuple-element.56) | copy-start | bytes 147460 | tf_op jit(solution)/shard_map/cond
  361.5 3.3 copy-start.12
  364.8 1.9 copy-start.35
  369.7 4.1 copy-start.34
  369.7 4.4 copy-start.30
  369.7 17.2 %copy-start.11 = (bf16[1,128,768]{2,1,0:T(8,128)(2,1)S(1)}, bf16[1,128,768]{2,1,0:T(8,128)(2,1)}, u32[]{:S(2)}) copy-start(bf16[1,128,768]{2,1,0:T(8,128)(2,1)} %param.35) | copy-start | bytes 589828
  388.5 108.5 %copy-start.15 = (bf16[192,768]{1,0:T(8,128)(2,1)S(1)}, bf16[192,768]{1,0:T(8,128)(2,1)}, u32[]{:S(2)}) copy-start(bf16[192,768]{1,0:T(8,128)(2,1)} %reduce-scatter.7.cloned.1.call-done) | copy-start | bytes 884740
Sparse Core Ops, SparseCore 0:
  9.6 33.6 all-gather.14
  47.0 44.2 all-gather.24
  94.0 42.9 all-gather.22
  138.5 16.2 all-gather.16
  156.2 37.4 all-gather.18
  195.1 37.4 all-gather.20
  234.8 44.3 all-gather.26
  281.3 43.2 all-gather.28
  327.8 24.7 reduce-scatter.6
  355.1 48.3 reduce-scatter.8
  406.0 47.8 reduce-scatter.10
  456.5 40.4 reduce-scatter.4
where the time goes:
time: 784 us; the launch traced here: 783 us
  blocking collectives  375 us (48%)
  waiting for transfers between devices  277 us (35%)
  matrix products  74.9 us (10%)
  local copies, waits for them, and re-layouts  28.5 us (4%)
  between operations  16.6 us (2%)
  other arithmetic  9.79 us (1%)
    psum x1, blocking collectives, shards(): lax.psum((owned[0], owned[1], owned[2], owned[3], owned[4], owned[5], own...  279 us
    reduce_scatter x1, waiting for transfers between devices, shards(): lax.psum_scatter(out_weight_grad.astype(jnp.bfloat16), 'fsdp', scatter_di...  50.4 us
    all_gather x1, waiting for transfers between devices, shards(): key_rows = lax.all_gather(key_flat, 'ctx', axis=1, tiled=True)  45.8 us
    reduce_scatter x1, waiting for transfers between devices, shards(): lax.psum_scatter(attn_weight_grad.astype(jnp.bfloat16), 'fsdp', scatter_d...  43 us
    all_gather x1, waiting for transfers between devices, shards(): lax.all_gather(fc_weight, 'fsdp', axis=0, tiled=True)  36.9 us
    all_gather x1, waiting for transfers between devices, shards(): lax.all_gather(out_weight, 'fsdp', axis=0, tiled=True)  35.7 us
    all_gather x1, waiting for transfers between devices, shards(): value_rows = lax.all_gather(value_flat, 'ctx', axis=1, tiled=True)  35.5 us
    all_gather x1, blocking collectives, shards(): lax.all_gather(log_totals, 'ctx', axis=2, tiled=True)  33 us
  transfers between devices with their start and end apart: 12, of which 9 were waited for; matrix products, arithmetic and copies ran while one was open for 14% of the time, Pallas kernels for 0%

commit v1 on v0

--- a/solution.py
+++ b/solution.py
@@ -9,6 +9,13 @@
 HD = 64
 LAYERS = 12
 EPSILON = 1e-05
+measure_stops_all = lambda local_block, shard_axis, x_in: jnp.split(
+    lax.all_gather(
+        jnp.concatenate([x_in, local_block], axis=0), tiled=True, axis_name=shard_axis, axis=1
+    ),
+    [x_in.shape[0]],
+    axis=0,
+)
 
 
 def layer_norm(values_in, norm_gain, norm_shift):
@@ -111,8 +118,7 @@
         jnp.zeros((seq_count, H, block_rows, HD), jnp.float32),
     )
     offset = jnp.int32(0)
-    key_rows = lax.all_gather(key_flat, "ctx", axis=1, tiled=True)
-    value_rows = lax.all_gather(value_flat, "ctx", axis=1, tiled=True)
+    key_rows, value_rows = measure_stops_all(value_flat, "ctx", key_flat)
     row_count = key_rows.shape[1]
 
     def update(running):

time: 784 us -> 848 us (1.082)
  waiting for transfers between devices: 277 us -> 343 us
    all_gather x2 -> x3, waiting for transfers between devices: 81.3 us -> 116 us  [the longest x1 49.7 us: lax.all_gather(jnp.concatenate([x_in, local_block], axis=0), tiled=True,...]
    reduce_scatter x1, waiting for transfers between devices: 10.9 us -> 29 us  [shards(): lax.psum_scatter(fc_weight_grad.astype(jnp.bfloat16), 'fsdp', scatter_dim...]
    all_gather x1, waiting for transfers between devices: 0.01 us -> 8.81 us  [shards(): lax.all_gather(grad_seq, 'ctx', axis=1, tiled=True)]
  transfers between devices with their start and end apart: 12 -> 13, of which waited for: 9 -> 12; matrix products, arithmetic and copies ran while one was open for 14% -> 12% of each run, Pallas kernels for 0% -> 0%
where the time goes in v1:
time: 848 us; the launch traced here: 844 us
  blocking collectives  373 us (44%)
  waiting for transfers between devices  343 us (40%)
  matrix products  67 us (8%)
  local copies, waits for them, and re-layouts  27.5 us (3%)
  between operations  16.5 us (2%)
  other arithmetic  15.7 us (2%)
    psum x1, blocking collectives, shards(): lax.psum((owned[0], owned[1], owned[2], owned[3], owned[4], owned[5], own...  279 us
    reduce_scatter x1, waiting for transfers between devices, shards(): lax.psum_scatter(out_weight_grad.astype(jnp.bfloat16), 'fsdp', scatter_di...  50.3 us
    all_gather x1, waiting for transfers between devices, lax.all_gather(jnp.concatenate([x_in, local_block], axis=0), tiled=True,...  49.7 us
    all_gather x1, waiting for transfers between devices, shards(): lax.all_gather(value_flat, 'ctx', axis=1, tiled=True)  45.2 us
    reduce_scatter x1, waiting for transfers between devices, shards(): lax.psum_scatter(attn_weight_grad.astype(jnp.bfloat16), 'fsdp', scatter_d...  43.2 us
    all_gather x1, waiting for transfers between devices, shards(): lax.all_gather(fc_weight, 'fsdp', axis=0, tiled=True)  36.9 us
    all_gather x1, waiting for transfers between devices, shards(): lax.all_gather(out_weight, 'fsdp', axis=0, tiled=True)  35.7 us
    all_gather x1, blocking collectives, shards(): lax.all_gather(deltas, 'ctx', axis=2, tiled=True)  32.9 us
  transfers between devices with their start and end apart: 13, of which 12 were waited for; matrix products, arithmetic and copies ran while one was open for 12% of the time, Pallas kernels for 0%

profile of v1, /device:TPU:0, one launch (start us, length us, event | category | flops | bytes accessed | tf_op | source)
XLA Modules:
  0.0 844.0 jit_solution(9345894214068369178)
XLA Ops:
  8.0 1.3 fusion.92
  10.0 0.8 dynamic-update-slice.1
  10.8 0.8 dynamic-update-slice
  11.6 0.8 dynamic-update-slice.2
  12.5 0.8 dynamic-update-slice.3
  13.3 0.8 dynamic-update-slice.4
  14.2 0.8 dynamic-update-slice.6
  15.0 0.8 dynamic-update-slice.5
  15.8 13.4 %all-reduce.19 = (bf16[768]{0:T(1024)(128)(2,1)S(1)}, bf16[768]{0:T(1024)(128)(2,1)S(1)}, bf16[768]{0:T(1024)(128)(2,1)S(1)}, bf16[768]{0:T(1024)(128)(2,1)S(1)}...) all-reduce(bf16[768]{0:T(1024)(128)(2,1)S(1)} %dynamic-update-slice, ...), channel_id=1, replica_groups=mesh['ctx'=8,'fsdp'=4] {'fsdp'}, use_global_device_ids=true, to_apply=%add.1 | all-reduce | flops 5376 | bytes 21504
  29.2 1.0 convert_reduce_fusion
  30.3 1.1 fusion.63
  31.4 11.8 %all-gather.16.cloned.1.call-done = bf16[768,2304]{1,0:T(8,128)(2,1)} async-done(((bf16[192,2304]{1,0:T(8,128)(2,1)}), bf16[768,2304]{1,0:T(8,128)(2,1)}) %all-gather.16.cloned.1.call-update) | async-done | bytes 3538960 | tf_op jit(solution)/shard_map/all_gather | solution.py:90
  43.2 2.8 fusion.85
  46.2 0.9 pad_maximum_fusion.1
  51.2 5.2 all-gather.5
  57.0 0.8 copy.49
  58.1 49.7 %all-gather.18.cloned.1.call-done = bf16[2,1024,768]{2,1,0:T(8,128)(2,1)} async-done(((bf16[2,128,768]{2,1,0:T(8,128)(2,1)}), bf16[2,1024,768]{2,1,0:T(8,128)(2,1)}) %all-gather.18.cloned.1.call-update) | async-done | bytes 3145744 | tf_op jit(solution)/shard_map/all_gather | solution.py:13
  107.8 11.9 %conditional.3 = (f32[1,12,128]{2,1,0:T(8,128)}, f32[1,12,128,64]{2,3,1,0:T(8,128)}, f32[1,12,128]{2,1,0:T(8,128)S(1)}) conditional(s32[]{:T(128)} %convert_element_type.215, () %tuple.32, (s32[]{:T(128)}, bf16[1,128,12,64]{1,3,2,0:T(8,128)(2,1)}, bf16[2,1024,768]{2,1,0:T(8,128)(2,1)}) %tuple.33), branch_computations={%region_2.0_spmd.clone, %region_3.6_spmd.clone} | conditional | flops 423233152 | bytes 35773468 | solution.py:141
  108.0 3.2 copy.58
  111.5 2.3 fusion.26
  113.8 2.6 fusion.28
  116.4 2.6 fusion.32
  120.3 1.0 fusion.71
  121.3 4.2 all-gather.20.cloned.1.call-done
  125.5 1.7 fusion.93
  127.5 36.9 %all-gather.22.cloned.1.call-done = bf16[768,3072]{1,0:T(8,128)(2,1)} async-done(((bf16[192,3072]{1,0:T(8,128)(2,1)}), bf16[768,3072]{1,0:T(8,128)(2,1)}) %all-gather.22.cloned.1.call-update) | async-done | bytes 4718608 | tf_op jit(solution)/shard_map/all_gather | solution.py:155
  164.4 3.2 convolution_add_fusion
  167.6 35.7 %all-gather.24.cloned.1.call-done = bf16[3072,768]{1,0:T(8,128)(2,1)} async-done(((bf16[768,768]{1,0:T(8,128)(2,1)}), bf16[3072,768]{1,0:T(8,128)(2,1)}) %all-gather.24.cloned.1.call-update) | async-done | bytes 4718608 | tf_op jit(solution)/shard_map/all_gather | solution.py:157
  203.3 5.1 fusion.94
  208.4 2.3 multiply_reduce_fusion
  210.7 1.0 fusion.90
  213.2 1.2 convolution_convert_fusion.4
  214.5 2.4 convolution_convert_fusion.3
  216.9 4.4 convolution_convert_fusion.1
  222.2 3.8 convolution_convert_fusion
  226.1 0.9 copy-done.8
  227.1 1.1 fusion.68
  228.2 21.3 %all-gather.26.cloned.1.call-done = bf16[1024,768]{1,0:T(8,128)(2,1)} async-done(((bf16[128,768]{1,0:T(8,128)(2,1)}), bf16[1024,768]{1,0:T(8,128)(2,1)}) %all-gather.26.cloned.1.call-update) | async-done | bytes 1572880 | tf_op jit(solution)/shard_map/all_gather | solution.py:268
  249.6 45.2 %all-gather.28.cloned.1.call-done = bf16[1024,768]{1,0:T(8,128)(2,1)} async-done(((bf16[128,768]{1,0:T(8,128)(2,1)}), bf16[1024,768]{1,0:T(8,128)(2,1)}) %all-gather.28.cloned.1.call-update) | async-done | bytes 1572880 | tf_op jit(solution)/shard_map/all_gather | solution.py:269
  294.8 17.9 %conditional.4 = (bf16[1,128,12,64]{1,3,2,0:T(8,128)(2,1)S(1)}) conditional(s32[]{:T(128)} %convert_element_type.215, () %tuple.34, (s32[]{:T(128)}, bf16[1,128,12,64]{1,3,2,0:T(8,128)(2,1)}, bf16[1,1024,768]{2,1,0:T(8,128)(2,1)}, f32[1,12,128]{2,1,0:T(8,128)}, bf16[1,128,12,64]{1,3,2,0:T(8,128)(2,1)}, /*index=5*/bf16[1,1024,768]{2,1,0:T(8,128)(2,1)}, ...), branch_computations={%region_11.12_spmd, %region_12.13_spmd} | conditional | flops 613744768 | bytes 25244712 | solution.py:263
  294.8 2.6 copy.52
  297.4 5.2 fusion.8
  302.6 0.8 iota_compare_fusion
  303.4 2.6 copy.53
  306.1 6.7 fusion.5
  312.7 32.0 %all_gather.77 = f32[1,12,1024]{2,1,0:T(8,128)} all-gather(f32[1,12,128]{2,1,0:T(8,128)} %copy-done.21), channel_id=1, replica_groups=mesh['ctx'=8,'fsdp'=4] {'ctx'}, dimensions={2}, use_global_device_ids=true | all-gather | bytes 55296 | tf_op jit(solution)/shard_map/all_gather | solution.py:196
  344.7 32.9 %all-gather.4 = f32[12,1024]{1,0:T(8,128)} all-gather(f32[12,128]{1,0:T(8,128)S(1)} %fusion.68), channel_id=6, replica_groups=mesh['ctx'=8,'fsdp'=4] {'ctx'}, dimensions={1}, use_global_device_ids=true | all-gather | bytes 55296 | tf_op jit(solution)/shard_map/all_gather | solution.py:197
  377.6 8.8 %all-gather.32.cloned.1.call-done = bf16[1024,768]{1,0:T(8,128)(2,1)} async-done(((bf16[128,768]{1,0:T(8,128)(2,1)}), bf16[1024,768]{1,0:T(8,128)(2,1)}) %all-gather.32.cloned.1.call-update) | async-done | bytes 1572880 | tf_op jit(solution)/shard_map/all_gather | solution.py:238
  386.5 19.1 %conditional.5 = (bf16[1,128,768]{1,2,0:T(8,128)(2,1)S(1)}, bf16[128,768]{0,1:T(8,128)(2,1)S(1)}) conditional(s32[]{:T(128)} %convert_element_type.242, () %tuple.36, (s32[]{:T(128)}, bf16[1,1024,768]{2,1,0:T(8,128)(2,1)}, bf16[128,768]{1,0:T(8,128)(2,1)S(1)}, f32[1,12,1024]{2,1,0:T(8,128)}, bf16[1,1024,768]{2,1,0:T(8,128)(2,1)}, ...), branch_computations={%region_13.14_spmd, %region_14.15_spmd} | conditional | flops 821362816 | bytes 65750148 | solution.py:227
  386.5 2.6 copy.56
  389.1 2.6 copy.54
  391.8 2.6 fusion.95
  394.6 2.0 fusion.13
  397.3 8.2 fusion.21
  405.6 3.0 convolution_convert_fusion.2
  410.4 3.6 reduce-scatter.7.cloned.1.call-done
  414.3 3.4 fusion.88
  418.8 10.5 %all-reduce.18 = (bf16[768]{0:T(1024)(128)(2,1)S(1)}, bf16[768]{0:T(1024)(128)(2,1)S(1)}, bf16[768]{0:T(1024)(128)(2,1)S(1)}, bf16[768]{0:T(1024)(128)(2,1)S(1)}...) all-reduce(bf16[768]{0:T(1024)(128)(2,1)S(1)} %dynamic-update-slice, ...), channel_id=1, replica_groups=mesh['ctx'=8,'fsdp'=4] {'fsdp'}, use_global_device_ids=true, to_apply=%add.7 | all-reduce | flops 9984 | bytes 39936
  429.6 1.9 fusion.70
  431.5 4.1 fusion.52
  435.7 29.0 %reduce-scatter.9.cloned.1.call-done = bf16[192,3072]{1,0:T(8,128)(2,1)} async-done(((bf16[768,3072]{1,0:T(8,128)(2,1)}), bf16[192,3072]{1,0:T(8,128)(2,1)}) %reduce-scatter.9.cloned.1.call-update) | async-done | bytes 1179664 | tf_op jit(solution)/shard_map/reduce_scatter | solution.py:316
  464.7 50.3 %reduce-scatter.11.cloned.1.call-done = bf16[768,768]{1,0:T(8,128)(2,1)} async-done(((bf16[3072,768]{1,0:T(8,128)(2,1)}), bf16[768,768]{1,0:T(8,128)(2,1)}) %reduce-scatter.11.cloned.1.call-update) | async-done | bytes 1179664 | tf_op jit(solution)/shard_map/reduce_scatter | solution.py:322
  515.0 43.2 %reduce-scatter.5.cloned.1.call-done = bf16[192,2304]{1,0:T(8,128)(2,1)} async-done(((bf16[768,2304]{1,0:T(8,128)(2,1)}), bf16[192,2304]{1,0:T(8,128)(2,1)}) %reduce-scatter.5.cloned.1.call-update) | async-done | bytes 884752 | tf_op jit(solution)/shard_map/reduce_scatter | solution.py:295
  558.2 279.0 %all-reduce.21 = (f32[192]{0:T(256)}, f32[192]{0:T(256)}, f32[192,2304]{1,0:T(8,128)}, f32[192]{0:T(256)}, f32[192]{0:T(256)}, /*index=5*/f32[192,768]{1,0:T(8,1...) all-reduce(f32[192]{0:T(256)S(1)} %get-tuple-element.210, ...), channel_id=1, replica_groups=mesh['ctx'=8,'fsdp'=4] {'ctx'}, use_global_device_ids=true, to_apply=%region_19.20 | all-reduce | flops 1771776 | bytes 10635264 | tf_op jit(solution)/shard_map/psum | solution.py:329
  (156 shorter events, 13.6 us)
Async XLA Ops:
  7.2 36.1 %all-gather.16.cloned.1.call-start = ((), (), s32[]{:S(2)}) async-start(), calls=%async_computation.4 | async-start | bytes 4423680 | tf_op jit(solution)/shard_map/all_gather | solution.py:90
  7.9 99.9 %all-gather.18.cloned.1.call-start = ((), (), s32[]{:S(2)}) async-start(), calls=%async_computation.5 | async-start | bytes 3538944 | tf_op jit(solution)/shard_map/all_gather | solution.py:13
  30.2 15.8 %copy-start.23 = (f32[128]{0:T(128)}, f32[128]{0:T(128)S(1)}, u32[]{:S(2)}) copy-start(f32[128]{0:T(128)S(1)} %broadcast_multiply_fusion.1) | copy-start | bytes 1540
  31.4 14.7 %copy-start.36 = (f32[128]{0:T(128)}, f32[128]{0:T(128)S(1)}, u32[]{:S(2)}) copy-start(f32[128]{0:T(128)S(1)} %fusion.63) | copy-start | bytes 1540
  31.4 14.7 %copy-start.26 = (f32[128]{0:T(128)}, f32[128]{0:T(128)S(1)}, u32[]{:S(2)}) copy-start(f32[128]{0:T(128)S(1)} %fusion.78) | copy-start | bytes 1540
  46.2 2.9 copy-start.4
  46.2 10.8 %copy-start.6 = (bf16[128,768]{1,0:T(8,128)(2,1)}, bf16[128,768]{1,0:T(8,128)(2,1)S(1)}, u32[]{:S(2)}) copy-start(bf16[128,768]{1,0:T(8,128)(2,1)S(1)} %get-tuple-element.193) | copy-start | bytes 589828
  47.1 78.4 %all-gather.20.cloned.1.call-start = ((), (), s32[]{:S(2)}) async-start(), calls=%async_computation.6 | async-start | bytes 1474560 | tf_op jit(solution)/shard_map/all_gather | solution.py:93
  47.8 3.4 copy-start.35
  47.9 116.5 %all-gather.22.cloned.1.call-start = ((), (), s32[]{:S(2)}) async-start(), calls=%async_computation.7 | async-start | bytes 5898240 | tf_op jit(solution)/shard_map/all_gather | solution.py:155
  48.4 154.9 %all-gather.24.cloned.1.call-start = ((), (), s32[]{:S(2)}) async-start(), calls=%async_computation.8 | async-start | bytes 5898240 | tf_op jit(solution)/shard_map/all_gather | solution.py:157
  49.0 200.5 %all-gather.26.cloned.1.call-start = ((), (), s32[]{:S(2)}) async-start(), calls=%async_computation.13 | async-start | bytes 1769472 | tf_op jit(solution)/shard_map/all_gather | solution.py:268
  49.8 245.0 %all-gather.28.cloned.1.call-start = ((), (), s32[]{:S(2)}) async-start(), calls=%async_computation.14 | async-start | bytes 1769472 | tf_op jit(solution)/shard_map/all_gather | solution.py:269
  50.6 327.1 %all-gather.30.cloned.1.call-start = ((), (), s32[]{:S(2)}) async-start(), calls=%async_computation.15 | async-start | bytes 1769472 | tf_op jit(solution)/shard_map/all_gather | solution.py:237
  57.8 328.6 %all-gather.32.cloned.1.call-start = ((), (), s32[]{:S(2)}) async-start(), calls=%async_computation.16 | async-start | bytes 1769472 | tf_op jit(solution)/shard_map/all_gather | solution.py:238
  107.8 17.7 %copy-start.1 = (bf16[1,128,768]{2,1,0:T(8,128)(2,1)S(1)}, bf16[1,128,768]{2,1,0:T(8,128)(2,1)}, u32[]{:S(2)}) copy-start(bf16[1,128,768]{2,1,0:T(8,128)(2,1)} %param.21) | copy-start | bytes 589828
  119.7 0.6 copy-start.21
  119.7 44.7 %copy-start.20 = (f32[4,1,768]{2,1,0:T(1,128)S(1)}, f32[4,1,768]{2,1,0:T(1,128)}, u32[]{:S(2)}) copy-start(f32[4,1,768]{2,1,0:T(1,128)} %convert_element_type.268) | copy-start | bytes 36868
  127.2 81.1 %copy-start.22 = (f32[128]{0:T(128)}, f32[128]{0:T(128)S(1)}, u32[]{:S(2)}) copy-start(f32[128]{0:T(128)S(1)} %broadcast_multiply_fusion) | copy-start | bytes 1540
  127.4 80.9 %copy-start.25 = (f32[128]{0:T(128)}, f32[128]{0:T(128)S(1)}, u32[]{:S(2)}) copy-start(f32[128]{0:T(128)S(1)} %fusion.79) | copy-start | bytes 1540
  164.4 38.9 %copy-start.10 = (bf16[1,128,768]{2,1,0:T(8,128)(2,1)S(1)}, bf16[1,128,768]{2,1,0:T(8,128)(2,1)}, u32[]{:S(2)}) copy-start(bf16[1,128,768]{2,1,0:T(8,128)(2,1)} %param.35) | copy-start | bytes 589828
  203.3 5.1 copy-start
  208.4 3.4 copy-start.11
  210.7 2.5 copy-start.3
  211.7 0.8 copy-start.33
  212.5 0.7 copy-start.9
  214.4 199.7 %reduce-scatter.7.cloned.1.call-start = ((), (), s32[]{:S(2)}) async-start(), calls=%async_computation.10 | async-start | bytes 1474560 | tf_op jit(solution)/shard_map/reduce_scatter | solution.py:304
  216.9 247.8 %reduce-scatter.9.cloned.1.call-start = ((), (), s32[]{:S(2)}) async-start(), calls=%async_computation.11 | async-start | bytes 5898240 | tf_op jit(solution)/shard_map/reduce_scatter | solution.py:316
  221.3 0.9 copy-start.12
  221.3 293.7 %reduce-scatter.11.cloned.1.call-start = ((), (), s32[]{:S(2)}) async-start(), calls=%async_computation.12 | async-start | bytes 5898240 | tf_op jit(solution)/shard_map/reduce_scatter | solution.py:322
  226.0 0.9 copy-start.8
  226.0 332.2 %reduce-scatter.5.cloned.1.call-start = ((), (), s32[]{:S(2)}) async-start(), calls=%async_computation.9 | async-start | bytes 4423680 | tf_op jit(solution)/shard_map/reduce_scatter | solution.py:295
  227.1 67.7 %copy-start.15 = (bf16[128,768]{0,1:T(8,128)(2,1)}, bf16[128,768]{0,1:T(8,128)(2,1)S(1)}, u32[]{:S(2)}) copy-start(bf16[128,768]{0,1:T(8,128)(2,1)S(1)} %copy.51) | copy-start | bytes 589828
  294.8 91.7 %copy-start.5 = (bf16[128,768]{1,0:T(8,128)(2,1)S(1)}, bf16[128,768]{1,0:T(8,128)(2,1)}, u32[]{:S(2)}) copy-start(bf16[128,768]{1,0:T(8,128)(2,1)} %copy-done.4) | copy-start | bytes 589828
  294.8 91.7 %copy-start.7 = (bf16[128,768]{1,0:T(8,128)(2,1)S(1)}, bf16[128,768]{1,0:T(8,128)(2,1)}, u32[]{:S(2)}) copy-start(bf16[128,768]{1,0:T(8,128)(2,1)} %slice.23) | copy-start | bytes 589828
  303.4 2.6 copy-start.16
  386.5 19.1 %copy-start.24 = (f32[128]{0:T(128)S(1)}, f32[128]{0:T(128)}, u32[]{:S(2)}) copy-start(f32[128]{0:T(128)} %copy-done.23) | copy-start | bytes 1540
  386.5 19.1 %copy-start.27 = (f32[128]{0:T(128)S(1)}, f32[128]{0:T(128)}, u32[]{:S(2)}) copy-start(f32[128]{0:T(128)} %copy-done.26) | copy-start | bytes 1540
  391.8 2.8 copy-start.13
  391.8 2.8 copy-start.19
  394.4 2.7 copy-start.2
  394.6 2.6 copy-start.18
  408.6 1.3 copy-start.38
  414.2 3.5 copy-start.37
  414.2 4.5 copy-start.28
  414.2 4.5 copy-start.29
  414.2 4.5 copy-start.30
  414.3 4.5 copy-start.31
  414.3 4.5 copy-start.32
  414.3 15.4 %copy-start.34 = (f32[128]{0:T(128)S(1)}, f32[128]{0:T(128)}, u32[]{:S(2)}) copy-start(f32[128]{0:T(128)} %copy-done.33) | copy-start | bytes 1540
  417.7 0.8 copy-start.14
  431.5 126.7 %copy-start.17 = (bf16[192,768]{1,0:T(8,128)(2,1)S(1)}, bf16[192,768]{1,0:T(8,128)(2,1)}, u32[]{:S(2)}) copy-start(bf16[192,768]{1,0:T(8,128)(2,1)} %reduce-scatter.7.cloned.1.call-done) | copy-start | bytes 884740
Sparse Core Ops, SparseCore 0:
  9.6 33.6 all-gather.15
  47.2 60.5 all-gather.17
  109.4 16.0 all-gather.19
  126.9 37.4 all-gather.21
  165.8 37.4 all-gather.23
  205.3 44.1 all-gather.25
  251.7 42.9 all-gather.27
  297.5 43.3 all-gather.29
  343.1 43.3 all-gather.31
  389.4 24.5 reduce-scatter.6
  416.8 47.8 reduce-scatter.8
  467.1 47.8 reduce-scatter.10
  517.7 40.4 reduce-scatter.4
